TPU v7x, 256 devices: a whole 4x4x8 slice. The times are simulated.
256 devices in a mesh: lon: 32 (over z_hi, y, core), lat: 8 (over x, z_lo).
Axes of the slice: x: 4, y: 4, z: 8 (z_hi: 4, z_lo: 2; z = z_hi * 2 + z_lo), core: 2. Of those that a mesh axis runs over, the one named last changes fastest.
Arguments:
- temp: float32 [16, 1024, 4096], P(None, 'lat', 'lon'), may hold values from -6 to 6
- salt: float32 [16, 1024, 4096], P(None, 'lat', 'lon'), may hold values from -6 to 6
- uvel: float32 [16, 1024, 4096], P(None, 'lat', 'lon'), may hold values from -6 to 6
- vvel: float32 [16, 1024, 4096], P(None, 'lat', 'lon'), may hold values from -6 to 6
- depth_levels: int32 [1024, 4096], P('lat', 'lon'), may hold values from 0 to 16
Outputs:
- temp_next: float32 [16, 1024, 4096], P(None, 'lat', 'lon')
- salt_next: float32 [16, 1024, 4096], P(None, 'lat', 'lon')
- uvel_next: float32 [16, 1024, 4096], P(None, 'lat', 'lon')
- vvel_next: float32 [16, 1024, 4096], P(None, 'lat', 'lon')
Inputs may be any that keep to these rules, and one draw needn't show every extreme that they name: `depth_levels`: wet levels are counted from the top.
All inputs are finite; a program needn't handle non-finite values.
Results may differ from a plain program's by a relative error of at most 0.0003.
Values sent between devices are 32-bit elements; how exact they have to be, the bound alone decides.
A program may use at most 128 MiB of HBM per device.

v0:
```python
import functools
import math

import jax
import jax.numpy as jnp
from jax import lax
from jax.experimental import pallas as pl
from jax.experimental.pallas import tpu as pltpu
from jax.sharding import PartitionSpec as P

time_step = 0.2
biharmonic = 0.01
signs = (1.0, 1.0, -1.0, -1.0)
top = 8


def when(cond, fn):
    if cond is True:
        fn()
    else:
        pl.when(cond)(fn)


def reverse_lanes(x):
    lane = lax.broadcasted_iota(jnp.int32, x.shape, 1)
    width = x.shape[1]
    bit = 1
    while bit < width:
        x = jnp.where((lane & bit) != 0, pltpu.roll(x, bit, 1), pltpu.roll(x, width - bit, 1))
        bit *= 2
    return x


def exchange_kernel(axes, nlat, nlon, t_hbm, s_hbm, u_hbm, v_hbm, d_hbm,
                    hs_o, hn_o, hw_o, he_o, cor_o,
                    xin, d_ref, top_b, bot_b, fold_b, lft_b, rgt_b, hs, hn, hw, he, cor,
                    send_sem, recv_sem, in_sem, local_sem):
    a = lax.axis_index("lat")
    b = lax.axis_index("lon")
    last = nlat - 1
    levels, rows, cols = t_hbm.shape
    left = (b + nlon - 1) % nlon
    right = (b + 1) % nlon
    mirror = nlon - 1 - b
    ne = (2 * nlon - 2 - b) % nlon
    nw = (nlon - b) % nlon
    fold = a == last
    loads = [pltpu.make_async_copy(src, xin.at[n], in_sem.at[n])
             for n, src in enumerate((t_hbm, s_hbm, u_hbm, v_hbm))]
    loads.append(pltpu.make_async_copy(d_hbm, d_ref, in_sem.at[4]))
    for copy in loads:
        copy.start()

    def dev(la, lo):
        return tuple(la if ax == "lat" else lo for ax in axes)

    def zero_south():
        hs[...] = jnp.zeros_like(hs)
        cor[0] = jnp.zeros_like(cor[0])
        cor[1] = jnp.zeros_like(cor[1])

    when(a == 0, zero_south)

    partners = [
        (a < last, (a + 1, b)), (a > 0, (a - 1, b)), (True, (a, left)), (True, (a, right)),
        (a < last, (a + 1, right)), (a < last, (a + 1, left)),
        (a > 0, (a - 1, right)), (a > 0, (a - 1, left)),
        (fold, (last, mirror)), (fold & (ne != b), (last, ne)), (fold & (nw != b), (last, nw)),
    ]
    barrier = pltpu.get_barrier_semaphore()
    for cond, target in partners:
        when(cond, lambda target=target: pl.semaphore_signal(
            barrier, 1, device_id=dev(*target), device_id_type=pl.DeviceIdType.MESH))

    for copy in loads:
        copy.wait()

    def rows_body(k, carry):
        wet = jnp.where(d_ref[...] > k, 1.0, 0.0).astype(jnp.float32)
        for n in range(4):
            x = xin[n, k] * wet
            top_b[n, k] = x[0:2]
            bot_b[n, k] = x[rows - 2:rows]
            flipped = reverse_lanes(x[rows - 8:rows])
            fold_b[n, k, 0:1] = signs[n] * flipped[7:8]
            fold_b[n, k, 1:2] = signs[n] * flipped[6:7]
        return carry

    def cols_body(k, carry):
        wet = jnp.where(d_ref[...] > k, 1.0, 0.0).astype(jnp.float32)
        for n in range(4):
            xt = jnp.transpose(xin[n, k] * wet)
            lft_b[n, k] = xt[0:2]
            rgt_b[n, k] = xt[cols - 2:cols]
        return carry

    lax.fori_loop(0, levels, rows_body, 0)

    below = (a + last) // (last + 1)
    above = (2 * last - a) // (last + 1)
    at_fold = a // last
    ne_apart = ((2 * b + 2) % nlon + nlon - 1) // nlon
    nw_apart = ((2 * b) % nlon + nlon - 1) // nlon
    peers = 2 + 3 * below + 3 * above + at_fold * (1 + ne_apart + nw_apart)
    pl.semaphore_wait(barrier, peers)

    relations = [
        (a < last, a > 0, bot_b, hs, (a + 1, b)),
        (a > 0, a < last, top_b, hn, (a - 1, b)),
        (fold, fold, fold_b, hn, (last, mirror)),
        (True, True, lft_b, he, (a, left)),
        (True, True, rgt_b, hw, (a, right)),
        (a < last, a > 0, rgt_b.at[:, :, 1:2], cor.at[0], (a + 1, right)),
        (a < last, a > 0, lft_b.at[:, :, 0:1], cor.at[1], (a + 1, left)),
        (a > 0, a < last, rgt_b.at[:, :, 1:2], cor.at[2], (a - 1, right)),
        (a > 0, a < last, lft_b.at[:, :, 0:1], cor.at[3], (a - 1, left)),
        (fold & (ne != b), fold & (ne != b), rgt_b.at[:, :, 1:2], cor.at[3], (last, ne)),
        (fold & (nw != b), fold & (nw != b), lft_b.at[:, :, 0:1], cor.at[2], (last, nw)),
    ]
    copies = []
    for idx, (send, recv, src, dst, target) in enumerate(relations):
        if idx == 3:
            lax.fori_loop(0, levels, cols_body, 0)
        copy = pltpu.make_async_remote_copy(
            src_ref=src, dst_ref=dst, send_sem=send_sem.at[idx], recv_sem=recv_sem.at[idx],
            device_id=dev(*target), device_id_type=pl.DeviceIdType.MESH)
        copies.append((send, recv, copy))
        when(send, copy.start)
    own = [
        (fold & (ne == b), pltpu.make_async_copy(rgt_b.at[:, :, 1:2], cor.at[3], local_sem.at[0])),
        (fold & (nw == b), pltpu.make_async_copy(lft_b.at[:, :, 0:1], cor.at[2], local_sem.at[1])),
    ]
    for cond, copy in own:
        when(cond, copy.start)
    for send, recv, copy in copies:
        when(send, copy.wait_send)
        when(recv, copy.wait_recv)
    for cond, copy in own:
        when(cond, copy.wait)
    hs_o[...] = hs[...]
    hn_o[...] = hn[...]
    hw_o[...] = hw[...]
    he_o[...] = he[...]
    cor_o[...] = cor[...]


def step_kernel(nlat, t_ref, s_ref, u_ref, v_ref, d_ref, f_ref, hs_ref, hn_ref, hw_ref, he_ref,
                cor_ref, to_ref, so_ref, uo_ref, vo_ref,
                base, vp1, vm1, vp2, vm2, accx, accy, mt, tf):
    step = pl.program_id(0)
    per_step = t_ref.shape[0]
    frame, width = base.shape[1], base.shape[2]
    rows = t_ref.shape[1]
    at_lat = lax.axis_index("lat")
    south = at_lat > 0
    fold = at_lat == nlat - 1

    @pl.when(step == 0)
    def _():
        base[...] = jnp.zeros_like(base)
        accx[...] = jnp.zeros_like(accx)
        accy[...] = jnp.zeros_like(accy)
        mt[...] = jnp.zeros_like(mt)
        tf[...] = jnp.zeros_like(tf)

    for sub in range(per_step):
        k = step * per_step + sub
        wet = jnp.where(d_ref[...] > k, 1.0, 0.0).astype(jnp.float32)
        lane = lax.broadcasted_iota(jnp.int32, (frame, width), 1)
        line_lane = lax.broadcasted_iota(jnp.int32, (1, width), 1)
        ins = (t_ref, s_ref, u_ref, v_ref)
        for n in range(4):
            base[n, top:top + rows, :] = ins[n][sub] * wet
            base[n, top - 2:top, :] = jnp.where(south, hs_ref[n, k], 0.0)
            base[n, top + rows:top + rows + 2, :] = hn_ref[n, k]
            mt[0:2] = he_ref[n, k]
            mt[width - 2:width] = hw_ref[n, k]
            tf[top:top + rows] = jnp.transpose(mt[...])
            nw_raw = cor_ref[2, n, k]
            ne_raw = cor_ref[3, n, k]
            sw_line = cor_ref[0, n, k]
            se_line = pltpu.roll(cor_ref[1, n, k], 1, 1)
            nw_line = pltpu.roll(cor_ref[2, n, k], width - 1, 1)
            ne_line = cor_ref[3, n, k]
            low = jnp.where(line_lane == width - 1, sw_line, jnp.where(line_lane == 0, se_line, 0.0))
            high = jnp.where(line_lane == width - 1, nw_line, jnp.where(line_lane == 0, ne_line, 0.0))
            tf[top - 1:top] = jnp.where(south, low, 0.0)
            mirrored = jnp.where(line_lane == width - 1, nw_raw,
                                 jnp.where(line_lane == 0, pltpu.roll(ne_raw, 1, 1), 0.0))
            tf[top + rows:top + rows + 1] = jnp.where(fold, signs[n] * mirrored, high)
            whole = base[n]
            edge = tf[...]
            vp1[n] = pltpu.roll(jnp.where(lane == 0, edge, whole), width - 1, 1)
            vm1[n] = pltpu.roll(jnp.where(lane == width - 1, edge, whole), 1, 1)
            vp2[n] = pltpu.roll(jnp.where(lane < 2, edge, whole), width - 2, 1)
            vm2[n] = pltpu.roll(jnp.where(lane >= width - 2, edge, whole), 2, 1)

        def at(ref, n, d):
            return ref[n, top + d:top + d + rows, :]

        centre = [at(base, n, 0) for n in range(4)]
        first, second = centre[2], centre[3]
        parts = []
        for n in range(4):
            east, west = at(vp1, n, 0), at(vm1, n, 0)
            north, south_ = at(base, n, 1), at(base, n, -1)
            carried = 0.5 * (first * (east - west) + second * (north - south_))
            smooth = (
                20.0 * centre[n]
                - 8.0 * (east + west + north + south_)
                + 2.0 * (at(vp1, n, 1) + at(vp1, n, -1) + at(vm1, n, 1) + at(vm1, n, -1))
                + at(base, n, 2) + at(base, n, -2) + at(vp2, n, 0) + at(vm2, n, 0)
            )
            parts.append((east, west, north, south_, carried, smooth))

        def density(a, b):
            return -0.2 * a + 0.8 * b

        dx = density(parts[0][0], parts[1][0]) - density(parts[0][1], parts[1][1])
        dy = density(parts[0][2], parts[1][2]) - density(parts[0][3], parts[1][3])
        totx = accx[...] + dx
        toty = accy[...] + dy
        accx[...] = totx
        accy[...] = toty
        grad_x = 0.5 * (totx - 0.5 * dx)
        grad_y = 0.5 * (toty - 0.5 * dy)
        coriolis = jnp.broadcast_to(f_ref[...], (rows, width))
        to_ref[sub] = (centre[0] - time_step * parts[0][4] - biharmonic * parts[0][5]) * wet
        so_ref[sub] = (centre[1] - time_step * parts[1][4] - biharmonic * parts[1][5]) * wet
        uo_ref[sub] = (
            first + time_step * (coriolis * second - grad_x - parts[2][4]) - biharmonic * parts[2][5]
        ) * wet
        vo_ref[sub] = (
            second + time_step * (-coriolis * first - grad_y - parts[3][4]) - biharmonic * parts[3][5]
        ) * wet


def shards(axes, temp, salt, uvel, vvel, depth_levels):
    levels, rows_dev, cols_dev = temp.shape
    nlat = lax.axis_size("lat")
    nlon = lax.axis_size("lon")
    at_lat = lax.axis_index("lat")
    f32 = jnp.float32
    vmem = pl.BlockSpec(memory_space=pltpu.VMEM)
    strip = jax.ShapeDtypeStruct((4, levels, 2, cols_dev), f32)
    corners = jax.ShapeDtypeStruct((4, 4, levels, 1, cols_dev), f32)
    hs, hn, hw, he, cor = pl.pallas_call(
        functools.partial(exchange_kernel, axes, nlat, nlon),
        out_shape=[strip] * 4 + [corners],
        in_specs=[pl.BlockSpec(memory_space=pl.ANY)] * 5,
        out_specs=[vmem] * 5,
        scratch_shapes=[pltpu.VMEM((4,) + temp.shape, f32),
                        pltpu.VMEM(depth_levels.shape, jnp.int32)]
        + [pltpu.VMEM(strip.shape, f32)] * 9
        + [pltpu.VMEM(corners.shape, f32)]
        + [pltpu.SemaphoreType.DMA((11,)), pltpu.SemaphoreType.DMA((11,)),
           pltpu.SemaphoreType.DMA((5,)), pltpu.SemaphoreType.DMA((2,))],
        compiler_params=pltpu.CompilerParams(collective_id=0, has_side_effects=True),
    )(temp, salt, uvel, vvel, depth_levels)

    total_rows = rows_dev * nlat
    global_rows = (at_lat * rows_dev + jnp.arange(rows_dev, dtype=jnp.int32)).astype(f32)
    coriolis = (0.5 * jnp.sin(math.pi * (global_rows + 0.5) / total_rows - 0.5 * math.pi))[:, None]

    frame = rows_dev + 2 * top
    per_step = 2
    level_block = pl.BlockSpec((per_step, rows_dev, cols_dev), lambda k: (k, 0, 0))
    plane = pl.BlockSpec((rows_dev, cols_dev), lambda k: (0, 0))
    column = pl.BlockSpec((rows_dev, 1), lambda k: (0, 0))
    out = pl.pallas_call(
        functools.partial(step_kernel, nlat),
        grid=(levels // per_step,),
        in_specs=[level_block] * 4 + [plane, column] + [vmem] * 5,
        out_specs=[level_block] * 4,
        out_shape=[jax.ShapeDtypeStruct(temp.shape, f32)] * 4,
        scratch_shapes=[pltpu.VMEM((4, frame, cols_dev), f32)] * 5
        + [pltpu.VMEM((rows_dev, cols_dev), f32)] * 2
        + [pltpu.VMEM((cols_dev, cols_dev), f32), pltpu.VMEM((frame, cols_dev), f32)],
        compiler_params=pltpu.CompilerParams(dimension_semantics=("arbitrary",)),
    )(temp, salt, uvel, vvel, depth_levels, coriolis, hs, hn, hw, he, cor)
    return tuple(out)


def solution(mesh):
    placed = (
        P(None, "lat", "lon"),
        P(None, "lat", "lon"),
        P(None, "lat", "lon"),
        P(None, "lat", "lon"),
        P("lat", "lon"),
    )
    return jax.shard_map(
        functools.partial(shards, tuple(mesh.axis_names)),
        mesh=mesh,
        in_specs=placed,
        out_specs=(
            P(None, "lat", "lon"),
            P(None, "lat", "lon"),
            P(None, "lat", "lon"),
            P(None, "lat", "lon"),
        ),
        check_vma=False,
    )
```

profile of v0, /device:TPU:32, one launch (start us, length us, event | category | flops | bytes accessed | tf_op | source)
XLA Modules:
  0.0 42.7 jit_solution(12728681446384185684)
XLA Ops:
  0.6 0.9 %sine_multiply_fusion.f_ref = f32[128,1]{1,0:T(8,128)} fusion(s32[]{:T(128)S(6)} %mul.16), kind=kLoop, calls=%fused_computation | loop fusion | flops 768 | bytes 516 | tf_op jit(solution)/shard_map/mul | solution.py:263
  1.5 27.7 %shard_map.84 = (f32[4,16,2,128]{3,2,1,0:T(2,128)}, f32[4,16,2,128]{3,2,1,0:T(2,128)}, f32[4,16,2,128]{3,2,1,0:T(2,128)}, f32[4,16,2,128]{3,2,1,0:T(2,128)}, f32[4,4,16,1,128]{4,3,2,1,0:T(1,128)}) custom-call(f32[16,128,128]{2,1,0:T(8,128)} %t_ref.1, f32[16,128,128]{2,1,0:T(8,128)} %s_ref.1, f32[16,128,128]{2,1,0:T(8,128)} %u_ref.1, f32[16,128,128]{2,1,0:T(8,128)} %v_ref.1, ...), custom_call_target="tpu_custom_call" | custom-call | tf_op jit(solution)/shard_map/pallas_call | solution.py:247
  29.2 13.5 %shard_map.85 = (f32[16,128,128]{2,1,0:T(8,128)}, f32[16,128,128]{2,1,0:T(8,128)}, f32[16,128,128]{2,1,0:T(8,128)}, f32[16,128,128]{2,1,0:T(8,128)}) custom-call(f32[16,128,128]{2,1,0:T(8,128)} %t_ref.1, f32[16,128,128]{2,1,0:T(8,128)} %s_ref.1, f32[16,128,128]{2,1,0:T(8,128)} %u_ref.1, f32[16,128,128]{2,1,0:T(8,128)} %v_ref.1, s32[128,128]{1,0:T(8,128)} %d_ref.1, ...), custom_call_target="tpu_custom_call" | custom-call | tf_op jit(solution)/shard_map/pallas_call | solution.py:270
where the time goes:
time: 42.8 us; the launch traced here: 42.7 us
  Pallas kernels  41.2 us (96%)
  other arithmetic  0.88 us (2%)
  between operations  0.64 us (1%)
    pallas_call x1, Pallas kernels, shards(): pl.pallas_call(functools.partial(exchange_kernel, axes, nlat, nlon), out_...  27.7 us
    pallas_call x1, Pallas kernels, shards(): pl.pallas_call(functools.partial(step_kernel, nlat), grid=(levels // per_...  13.5 us
    mul x1, other arithmetic, shards(): 0.5 * jnp.sin(math.pi * (global_rows + 0.5) / total_rows - 0.5 * math.pi)  0.88 us

commit v1 on v0

--- a/solution.py
+++ b/solution.py
@@ -263,7 +263,7 @@
     coriolis = (0.5 * jnp.sin(math.pi * (global_rows + 0.5) / total_rows - 0.5 * math.pi))[:, None]
 
     frame = rows_dev + 2 * top
-    per_step = 2
+    per_step = 4
     level_block = pl.BlockSpec((per_step, rows_dev, cols_dev), lambda k: (k, 0, 0))
     plane = pl.BlockSpec((rows_dev, cols_dev), lambda k: (0, 0))
     column = pl.BlockSpec((rows_dev, 1), lambda k: (0, 0))

time: 42.8 us -> 42.2 us (0.986)
  Pallas kernels: 41.2 us -> 40.5 us
    pallas_call x1, Pallas kernels: 13.5 us -> 12.9 us  [shards(): pl.pallas_call(functools.partial(step_kernel, nlat), grid=(levels // per_...]
where the time goes in v1:
time: 42.2 us; the launch traced here: 42.1 us
  Pallas kernels  40.5 us (96%)
  other arithmetic  0.88 us (2%)
  between operations  0.64 us (2%)
    pallas_call x1, Pallas kernels, shards(): pl.pallas_call(functools.partial(exchange_kernel, axes, nlat, nlon), out_...  27.7 us
    pallas_call x1, Pallas kernels, shards(): pl.pallas_call(functools.partial(step_kernel, nlat), grid=(levels // per_...  12.9 us
    mul x1, other arithmetic, shards(): 0.5 * jnp.sin(math.pi * (global_rows + 0.5) / total_rows - 0.5 * math.pi)  0.88 us

profile of v1, /device:TPU:32, one launch (start us, length us, event | category | flops | bytes accessed | tf_op | source)
XLA Modules:
  0.0 42.1 jit_solution(15328185985838522000)
XLA Ops:
  0.6 0.9 %sine_multiply_fusion.f_ref = f32[128,1]{1,0:T(8,128)} fusion(s32[]{:T(128)S(6)} %mul.16), kind=kLoop, calls=%fused_computation | loop fusion | flops 768 | bytes 516 | tf_op jit(solution)/shard_map/mul | solution.py:263
  1.5 27.7 %shard_map.84 = (f32[4,16,2,128]{3,2,1,0:T(2,128)}, f32[4,16,2,128]{3,2,1,0:T(2,128)}, f32[4,16,2,128]{3,2,1,0:T(2,128)}, f32[4,16,2,128]{3,2,1,0:T(2,128)}, f32[4,4,16,1,128]{4,3,2,1,0:T(1,128)}) custom-call(f32[16,128,128]{2,1,0:T(8,128)} %t_ref.1, f32[16,128,128]{2,1,0:T(8,128)} %s_ref.1, f32[16,128,128]{2,1,0:T(8,128)} %u_ref.1, f32[16,128,128]{2,1,0:T(8,128)} %v_ref.1, ...), custom_call_target="tpu_custom_call" | custom-call | tf_op jit(solution)/shard_map/pallas_call | solution.py:247
  29.2 12.9 %shard_map.85 = (f32[16,128,128]{2,1,0:T(8,128)}, f32[16,128,128]{2,1,0:T(8,128)}, f32[16,128,128]{2,1,0:T(8,128)}, f32[16,128,128]{2,1,0:T(8,128)}) custom-call(f32[16,128,128]{2,1,0:T(8,128)} %t_ref.1, f32[16,128,128]{2,1,0:T(8,128)} %s_ref.1, f32[16,128,128]{2,1,0:T(8,128)} %u_ref.1, f32[16,128,128]{2,1,0:T(8,128)} %v_ref.1, s32[128,128]{1,0:T(8,128)} %d_ref.1, ...), custom_call_target="tpu_custom_call" | custom-call | tf_op jit(solution)/shard_map/pallas_call | solution.py:270

commit v2 on v1

--- a/solution.py
+++ b/solution.py
@@ -86,12 +86,26 @@
             fold_b[n, k, 1:2] = signs[n] * flipped[6:7]
         return carry
 
-    def cols_body(k, carry):
-        wet = jnp.where(d_ref[...] > k, 1.0, 0.0).astype(jnp.float32)
-        for n in range(4):
-            xt = jnp.transpose(xin[n, k] * wet)
-            lft_b[n, k] = xt[0:2]
-            rgt_b[n, k] = xt[cols - 2:cols]
+    group = cols // 16
+
+    def cols_body(g, carry):
+        lane = lax.broadcasted_iota(jnp.int32, (rows, cols), 1)
+        packed = jnp.zeros((rows, cols), jnp.float32)
+        for kk in range(group):
+            k = g * group + kk
+            wet = jnp.where(d_ref[...] > k, 1.0, 0.0).astype(jnp.float32)
+            for n in range(4):
+                slot = 16 * kk + 4 * n
+                x = xin[n, k] * wet
+                packed = jnp.where((lane >= slot) & (lane < slot + 4),
+                                   pltpu.roll(x, (slot + 2) % cols, 1), packed)
+        pt = jnp.transpose(packed)
+        for kk in range(group):
+            k = g * group + kk
+            for n in range(4):
+                slot = 16 * kk + 4 * n
+                rgt_b[n, k] = pt[slot:slot + 2]
+                lft_b[n, k] = pt[slot + 2:slot + 4]
         return carry
 
     lax.fori_loop(0, levels, rows_body, 0)
@@ -120,7 +134,7 @@
     copies = []
     for idx, (send, recv, src, dst, target) in enumerate(relations):
         if idx == 3:
-            lax.fori_loop(0, levels, cols_body, 0)
+            lax.fori_loop(0, levels // group, cols_body, 0)
         copy = pltpu.make_async_remote_copy(
             src_ref=src, dst_ref=dst, send_sem=send_sem.at[idx], recv_sem=recv_sem.at[idx],
             device_id=dev(*target), device_id_type=pl.DeviceIdType.MESH)

time: 42.2 us -> 41.9 us (level)
  no operation moved by 1% of the time
where the time goes in v2:
time: 41.9 us; the launch traced here: 41.8 us
  Pallas kernels  40.3 us (96%)
  other arithmetic  0.88 us (2%)
  between operations  0.64 us (2%)
    pallas_call x1, Pallas kernels, shards(): pl.pallas_call(functools.partial(exchange_kernel, axes, nlat, nlon), out_...  27.4 us
    pallas_call x1, Pallas kernels, shards(): pl.pallas_call(functools.partial(step_kernel, nlat), grid=(levels // per_...  12.9 us
    mul x1, other arithmetic, shards(): 0.5 * jnp.sin(math.pi * (global_rows + 0.5) / total_rows - 0.5 * math.pi)  0.88 us

profile of v2, /device:TPU:32, one launch (start us, length us, event | category | flops | bytes accessed | tf_op | source)
XLA Modules:
  0.0 41.8 jit_solution(6568725111650287015)
XLA Ops:
  0.6 0.9 %sine_multiply_fusion.f_ref = f32[128,1]{1,0:T(8,128)} fusion(s32[]{:T(128)S(6)} %mul.16), kind=kLoop, calls=%fused_computation | loop fusion | flops 768 | bytes 516 | tf_op jit(solution)/shard_map/mul | solution.py:277
  1.5 27.4 %shard_map.84 = (f32[4,16,2,128]{3,2,1,0:T(2,128)}, f32[4,16,2,128]{3,2,1,0:T(2,128)}, f32[4,16,2,128]{3,2,1,0:T(2,128)}, f32[4,16,2,128]{3,2,1,0:T(2,128)}, f32[4,4,16,1,128]{4,3,2,1,0:T(1,128)}) custom-call(f32[16,128,128]{2,1,0:T(8,128)} %t_ref.1, f32[16,128,128]{2,1,0:T(8,128)} %s_ref.1, f32[16,128,128]{2,1,0:T(8,128)} %u_ref.1, f32[16,128,128]{2,1,0:T(8,128)} %v_ref.1, ...), custom_call_target="tpu_custom_call" | custom-call | tf_op jit(solution)/shard_map/pallas_call | solution.py:261
  29.0 12.9 %shard_map.85 = (f32[16,128,128]{2,1,0:T(8,128)}, f32[16,128,128]{2,1,0:T(8,128)}, f32[16,128,128]{2,1,0:T(8,128)}, f32[16,128,128]{2,1,0:T(8,128)}) custom-call(f32[16,128,128]{2,1,0:T(8,128)} %t_ref.1, f32[16,128,128]{2,1,0:T(8,128)} %s_ref.1, f32[16,128,128]{2,1,0:T(8,128)} %u_ref.1, f32[16,128,128]{2,1,0:T(8,128)} %v_ref.1, s32[128,128]{1,0:T(8,128)} %d_ref.1, ...), custom_call_target="tpu_custom_call" | custom-call | tf_op jit(solution)/shard_map/pallas_call | solution.py:284

commit v3 on v2

--- a/solution.py
+++ b/solution.py
@@ -33,7 +33,7 @@
 
 def exchange_kernel(axes, nlat, nlon, t_hbm, s_hbm, u_hbm, v_hbm, d_hbm,
                     hs_o, hn_o, hw_o, he_o, cor_o,
-                    xin, d_ref, top_b, bot_b, fold_b, lft_b, rgt_b, hs, hn, hw, he, cor,
+                    xin, d_ref, top_b, bot_b, fold_b, lft_b, rgt_b, lc, rc, hs, hn, hw, he, cor,
                     send_sem, recv_sem, in_sem, local_sem):
     a = lax.axis_index("lat")
     b = lax.axis_index("lon")
@@ -60,6 +60,8 @@
         cor[1] = jnp.zeros_like(cor[1])
 
     when(a == 0, zero_south)
+    lc[...] = jnp.zeros_like(lc)
+    rc[...] = jnp.zeros_like(rc)
 
     partners = [
         (a < last, (a + 1, b)), (a > 0, (a - 1, b)), (True, (a, left)), (True, (a, right)),
@@ -79,11 +81,11 @@
         wet = jnp.where(d_ref[...] > k, 1.0, 0.0).astype(jnp.float32)
         for n in range(4):
             x = xin[n, k] * wet
-            top_b[n, k] = x[0:2]
-            bot_b[n, k] = x[rows - 2:rows]
+            top_b[k, 2 * n:2 * n + 2] = x[0:2]
+            bot_b[k, 2 * n:2 * n + 2] = x[rows - 2:rows]
             flipped = reverse_lanes(x[rows - 8:rows])
-            fold_b[n, k, 0:1] = signs[n] * flipped[7:8]
-            fold_b[n, k, 1:2] = signs[n] * flipped[6:7]
+            fold_b[k, 2 * n:2 * n + 1] = signs[n] * flipped[7:8]
+            fold_b[k, 2 * n + 1:2 * n + 2] = signs[n] * flipped[6:7]
         return carry
 
     group = cols // 16
@@ -104,8 +106,10 @@
             k = g * group + kk
             for n in range(4):
                 slot = 16 * kk + 4 * n
-                rgt_b[n, k] = pt[slot:slot + 2]
-                lft_b[n, k] = pt[slot + 2:slot + 4]
+                rgt_b[k, 2 * n:2 * n + 2] = pt[slot:slot + 2]
+                lft_b[k, 2 * n:2 * n + 2] = pt[slot + 2:slot + 4]
+                rc[k, n:n + 1] = pt[slot + 1:slot + 2]
+                lc[k, n:n + 1] = pt[slot + 2:slot + 3]
         return carry
 
     lax.fori_loop(0, levels, rows_body, 0)
@@ -124,12 +128,12 @@
         (fold, fold, fold_b, hn, (last, mirror)),
         (True, True, lft_b, he, (a, left)),
         (True, True, rgt_b, hw, (a, right)),
-        (a < last, a > 0, rgt_b.at[:, :, 1:2], cor.at[0], (a + 1, right)),
-        (a < last, a > 0, lft_b.at[:, :, 0:1], cor.at[1], (a + 1, left)),
-        (a > 0, a < last, rgt_b.at[:, :, 1:2], cor.at[2], (a - 1, right)),
-        (a > 0, a < last, lft_b.at[:, :, 0:1], cor.at[3], (a - 1, left)),
-        (fold & (ne != b), fold & (ne != b), rgt_b.at[:, :, 1:2], cor.at[3], (last, ne)),
-        (fold & (nw != b), fold & (nw != b), lft_b.at[:, :, 0:1], cor.at[2], (last, nw)),
+        (a < last, a > 0, rc, cor.at[0], (a + 1, right)),
+        (a < last, a > 0, lc, cor.at[1], (a + 1, left)),
+        (a > 0, a < last, rc, cor.at[2], (a - 1, right)),
+        (a > 0, a < last, lc, cor.at[3], (a - 1, left)),
+        (fold & (ne != b), fold & (ne != b), rc, cor.at[3], (last, ne)),
+        (fold & (nw != b), fold & (nw != b), lc, cor.at[2], (last, nw)),
     ]
     copies = []
     for idx, (send, recv, src, dst, target) in enumerate(relations):
@@ -141,8 +145,8 @@
         copies.append((send, recv, copy))
         when(send, copy.start)
     own = [
-        (fold & (ne == b), pltpu.make_async_copy(rgt_b.at[:, :, 1:2], cor.at[3], local_sem.at[0])),
-        (fold & (nw == b), pltpu.make_async_copy(lft_b.at[:, :, 0:1], cor.at[2], local_sem.at[1])),
+        (fold & (ne == b), pltpu.make_async_copy(rc, cor.at[3], local_sem.at[0])),
+        (fold & (nw == b), pltpu.make_async_copy(lc, cor.at[2], local_sem.at[1])),
     ]
     for cond, copy in own:
         when(cond, copy.start)
@@ -185,17 +189,17 @@
         ins = (t_ref, s_ref, u_ref, v_ref)
         for n in range(4):
             base[n, top:top + rows, :] = ins[n][sub] * wet
-            base[n, top - 2:top, :] = jnp.where(south, hs_ref[n, k], 0.0)
-            base[n, top + rows:top + rows + 2, :] = hn_ref[n, k]
-            mt[0:2] = he_ref[n, k]
-            mt[width - 2:width] = hw_ref[n, k]
+            base[n, top - 2:top, :] = jnp.where(south, hs_ref[k, 2 * n:2 * n + 2], 0.0)
+            base[n, top + rows:top + rows + 2, :] = hn_ref[k, 2 * n:2 * n + 2]
+            mt[0:2] = he_ref[k, 2 * n:2 * n + 2]
+            mt[width - 2:width] = hw_ref[k, 2 * n:2 * n + 2]
             tf[top:top + rows] = jnp.transpose(mt[...])
-            nw_raw = cor_ref[2, n, k]
-            ne_raw = cor_ref[3, n, k]
-            sw_line = cor_ref[0, n, k]
-            se_line = pltpu.roll(cor_ref[1, n, k], 1, 1)
-            nw_line = pltpu.roll(cor_ref[2, n, k], width - 1, 1)
-            ne_line = cor_ref[3, n, k]
+            nw_raw = cor_ref[2, k, n:n + 1]
+            ne_raw = cor_ref[3, k, n:n + 1]
+            sw_line = cor_ref[0, k, n:n + 1]
+            se_line = pltpu.roll(cor_ref[1, k, n:n + 1], 1, 1)
+            nw_line = pltpu.roll(nw_raw, width - 1, 1)
+            ne_line = ne_raw
             low = jnp.where(line_lane == width - 1, sw_line, jnp.where(line_lane == 0, se_line, 0.0))
             high = jnp.where(line_lane == width - 1, nw_line, jnp.where(line_lane == 0, ne_line, 0.0))
             tf[top - 1:top] = jnp.where(south, low, 0.0)
@@ -256,8 +260,8 @@
     at_lat = lax.axis_index("lat")
     f32 = jnp.float32
     vmem = pl.BlockSpec(memory_space=pltpu.VMEM)
-    strip = jax.ShapeDtypeStruct((4, levels, 2, cols_dev), f32)
-    corners = jax.ShapeDtypeStruct((4, 4, levels, 1, cols_dev), f32)
+    strip = jax.ShapeDtypeStruct((levels, 8, cols_dev), f32)
+    corners = jax.ShapeDtypeStruct((4, levels, 8, cols_dev), f32)
     hs, hn, hw, he, cor = pl.pallas_call(
         functools.partial(exchange_kernel, axes, nlat, nlon),
         out_shape=[strip] * 4 + [corners],
@@ -265,7 +269,7 @@
         out_specs=[vmem] * 5,
         scratch_shapes=[pltpu.VMEM((4,) + temp.shape, f32),
                         pltpu.VMEM(depth_levels.shape, jnp.int32)]
-        + [pltpu.VMEM(strip.shape, f32)] * 9
+        + [pltpu.VMEM(strip.shape, f32)] * 11
         + [pltpu.VMEM(corners.shape, f32)]
         + [pltpu.SemaphoreType.DMA((11,)), pltpu.SemaphoreType.DMA((11,)),
            pltpu.SemaphoreType.DMA((5,)), pltpu.SemaphoreType.DMA((2,))],

time: 41.9 us -> 44.9 us (1.072)
  Pallas kernels: 40.3 us -> 43.2 us
    pallas_call x1, Pallas kernels: 27.4 us -> 30 us  [shards(): pl.pallas_call(functools.partial(exchange_kernel, axes, nlat, nlon), out_...]
where the time goes in v3:
time: 44.9 us; the launch traced here: 44.7 us
  Pallas kernels  43.2 us (96%)
  other arithmetic  0.87 us (2%)
  between operations  0.64 us (1%)
    pallas_call x1, Pallas kernels, shards(): pl.pallas_call(functools.partial(exchange_kernel, axes, nlat, nlon), out_...  30 us
    pallas_call x1, Pallas kernels, shards(): pl.pallas_call(functools.partial(step_kernel, nlat), grid=(levels // per_...  13.2 us

profile of v3, /device:TPU:32, one launch (start us, length us, event | category | flops | bytes accessed | tf_op | source)
XLA Modules:
  0.0 44.7 jit_solution(9101395883773935382)
XLA Ops:
  0.6 0.9 %sine_multiply_fusion.f_ref = f32[128,1]{1,0:T(8,128)} fusion(s32[]{:T(128)S(6)} %mul.16), kind=kLoop, calls=%fused_computation | loop fusion | flops 768 | bytes 516 | tf_op jit(solution)/shard_map/mul | solution.py:281
  1.5 30.0 %shard_map.84 = (f32[16,8,128]{2,1,0:T(8,128)}, f32[16,8,128]{2,1,0:T(8,128)}, f32[16,8,128]{2,1,0:T(8,128)}, f32[16,8,128]{2,1,0:T(8,128)}, f32[4,16,8,128]{3,2,1,0:T(8,128)}) custom-call(f32[16,128,128]{2,1,0:T(8,128)} %t_ref.1, f32[16,128,128]{2,1,0:T(8,128)} %s_ref.1, f32[16,128,128]{2,1,0:T(8,128)} %u_ref.1, f32[16,128,128]{2,1,0:T(8,128)} %v_ref.1, ...), custom_call_target="tpu_custom_call" | custom-call | tf_op jit(solution)/shard_map/pallas_call | solution.py:265
  31.5 13.2 %shard_map.85 = (f32[16,128,128]{2,1,0:T(8,128)}, f32[16,128,128]{2,1,0:T(8,128)}, f32[16,128,128]{2,1,0:T(8,128)}, f32[16,128,128]{2,1,0:T(8,128)}) custom-call(f32[16,128,128]{2,1,0:T(8,128)} %t_ref.1, f32[16,128,128]{2,1,0:T(8,128)} %s_ref.1, f32[16,128,128]{2,1,0:T(8,128)} %u_ref.1, f32[16,128,128]{2,1,0:T(8,128)} %v_ref.1, s32[128,128]{1,0:T(8,128)} %d_ref.1, ...), custom_call_target="tpu_custom_call" | custom-call | tf_op jit(solution)/shard_map/pallas_call | solution.py:288

commit v4 on v2

--- a/solution.py
+++ b/solution.py
@@ -33,7 +33,7 @@
 
 def exchange_kernel(axes, nlat, nlon, t_hbm, s_hbm, u_hbm, v_hbm, d_hbm,
                     hs_o, hn_o, hw_o, he_o, cor_o,
-                    xin, d_ref, top_b, bot_b, fold_b, lft_b, rgt_b, hs, hn, hw, he, cor,
+                    xin, d_ref, top_b, bot_b, fold_b, lft_b, rgt_b, hs, hn, hw, he, csrc, cor,
                     send_sem, recv_sem, in_sem, local_sem):
     a = lax.axis_index("lat")
     b = lax.axis_index("lon")
@@ -60,6 +60,7 @@
         cor[1] = jnp.zeros_like(cor[1])
 
     when(a == 0, zero_south)
+    csrc[...] = jnp.zeros_like(csrc)
 
     partners = [
         (a < last, (a + 1, b)), (a > 0, (a - 1, b)), (True, (a, left)), (True, (a, right)),
@@ -100,6 +101,8 @@
                 packed = jnp.where((lane >= slot) & (lane < slot + 4),
                                    pltpu.roll(x, (slot + 2) % cols, 1), packed)
         pt = jnp.transpose(packed)
+        csrc[g, 0:1] = packed[0:1]
+        csrc[g, 1:2] = packed[rows - 1:rows]
         for kk in range(group):
             k = g * group + kk
             for n in range(4):
@@ -124,12 +127,12 @@
         (fold, fold, fold_b, hn, (last, mirror)),
         (True, True, lft_b, he, (a, left)),
         (True, True, rgt_b, hw, (a, right)),
-        (a < last, a > 0, rgt_b.at[:, :, 1:2], cor.at[0], (a + 1, right)),
-        (a < last, a > 0, lft_b.at[:, :, 0:1], cor.at[1], (a + 1, left)),
-        (a > 0, a < last, rgt_b.at[:, :, 1:2], cor.at[2], (a - 1, right)),
-        (a > 0, a < last, lft_b.at[:, :, 0:1], cor.at[3], (a - 1, left)),
-        (fold & (ne != b), fold & (ne != b), rgt_b.at[:, :, 1:2], cor.at[3], (last, ne)),
-        (fold & (nw != b), fold & (nw != b), lft_b.at[:, :, 0:1], cor.at[2], (last, nw)),
+        (a < last, a > 0, csrc, cor.at[0], (a + 1, right)),
+        (a < last, a > 0, csrc, cor.at[1], (a + 1, left)),
+        (a > 0, a < last, csrc, cor.at[2], (a - 1, right)),
+        (a > 0, a < last, csrc, cor.at[3], (a - 1, left)),
+        (fold & (ne != b), fold & (ne != b), csrc, cor.at[3], (last, ne)),
+        (fold & (nw != b), fold & (nw != b), csrc, cor.at[2], (last, nw)),
     ]
     copies = []
     for idx, (send, recv, src, dst, target) in enumerate(relations):
@@ -141,8 +144,8 @@
         copies.append((send, recv, copy))
         when(send, copy.start)
     own = [
-        (fold & (ne == b), pltpu.make_async_copy(rgt_b.at[:, :, 1:2], cor.at[3], local_sem.at[0])),
-        (fold & (nw == b), pltpu.make_async_copy(lft_b.at[:, :, 0:1], cor.at[2], local_sem.at[1])),
+        (fold & (ne == b), pltpu.make_async_copy(csrc, cor.at[3], local_sem.at[0])),
+        (fold & (nw == b), pltpu.make_async_copy(csrc, cor.at[2], local_sem.at[1])),
     ]
     for cond, copy in own:
         when(cond, copy.start)
@@ -190,17 +193,22 @@
             mt[0:2] = he_ref[n, k]
             mt[width - 2:width] = hw_ref[n, k]
             tf[top:top + rows] = jnp.transpose(mt[...])
-            nw_raw = cor_ref[2, n, k]
-            ne_raw = cor_ref[3, n, k]
-            sw_line = cor_ref[0, n, k]
-            se_line = pltpu.roll(cor_ref[1, n, k], 1, 1)
-            nw_line = pltpu.roll(cor_ref[2, n, k], width - 1, 1)
-            ne_line = cor_ref[3, n, k]
+            slot = 16 * sub + 4 * n
+
+            def to_lane(line, src, dst):
+                return pltpu.roll(line, (dst - src) % width, 1)
+
+            sw_line = to_lane(cor_ref[0, step, 1:2], slot + 1, width - 1)
+            se_line = to_lane(cor_ref[1, step, 1:2], slot + 2, 0)
+            nw_line = to_lane(cor_ref[2, step, 0:1], slot + 1, width - 1)
+            ne_line = to_lane(cor_ref[3, step, 0:1], slot + 2, 0)
+            nw_raw = to_lane(cor_ref[2, step, 1:2], slot + 2, width - 1)
+            ne_raw = to_lane(cor_ref[3, step, 1:2], slot + 1, 0)
             low = jnp.where(line_lane == width - 1, sw_line, jnp.where(line_lane == 0, se_line, 0.0))
             high = jnp.where(line_lane == width - 1, nw_line, jnp.where(line_lane == 0, ne_line, 0.0))
             tf[top - 1:top] = jnp.where(south, low, 0.0)
             mirrored = jnp.where(line_lane == width - 1, nw_raw,
-                                 jnp.where(line_lane == 0, pltpu.roll(ne_raw, 1, 1), 0.0))
+                                 jnp.where(line_lane == 0, ne_raw, 0.0))
             tf[top + rows:top + rows + 1] = jnp.where(fold, signs[n] * mirrored, high)
             whole = base[n]
             edge = tf[...]
@@ -257,7 +265,7 @@
     f32 = jnp.float32
     vmem = pl.BlockSpec(memory_space=pltpu.VMEM)
     strip = jax.ShapeDtypeStruct((4, levels, 2, cols_dev), f32)
-    corners = jax.ShapeDtypeStruct((4, 4, levels, 1, cols_dev), f32)
+    corners = jax.ShapeDtypeStruct((4, levels * 16 // cols_dev, 8, cols_dev), f32)
     hs, hn, hw, he, cor = pl.pallas_call(
         functools.partial(exchange_kernel, axes, nlat, nlon),
         out_shape=[strip] * 4 + [corners],
@@ -266,7 +274,7 @@
         scratch_shapes=[pltpu.VMEM((4,) + temp.shape, f32),
                         pltpu.VMEM(depth_levels.shape, jnp.int32)]
         + [pltpu.VMEM(strip.shape, f32)] * 9
-        + [pltpu.VMEM(corners.shape, f32)]
+        + [pltpu.VMEM(corners.shape[1:], f32), pltpu.VMEM(corners.shape, f32)]
         + [pltpu.SemaphoreType.DMA((11,)), pltpu.SemaphoreType.DMA((11,)),
            pltpu.SemaphoreType.DMA((5,)), pltpu.SemaphoreType.DMA((2,))],
         compiler_params=pltpu.CompilerParams(collective_id=0, has_side_effects=True),
@@ -277,7 +285,7 @@
     coriolis = (0.5 * jnp.sin(math.pi * (global_rows + 0.5) / total_rows - 0.5 * math.pi))[:, None]
 
     frame = rows_dev + 2 * top
-    per_step = 4
+    per_step = cols_dev // 16
     level_block = pl.BlockSpec((per_step, rows_dev, cols_dev), lambda k: (k, 0, 0))
     plane = pl.BlockSpec((rows_dev, cols_dev), lambda k: (0, 0))
     column = pl.BlockSpec((rows_dev, 1), lambda k: (0, 0))

time: 41.9 us -> 41.4 us (0.988)
  Pallas kernels: 40.3 us -> 39.8 us
    pallas_call x1, Pallas kernels: 27.4 us -> 25.5 us  [shards(): pl.pallas_call(functools.partial(exchange_kernel, axes, nlat, nlon), out_...]
    pallas_call x1, Pallas kernels: 12.9 us -> 14.3 us  [shards(): pl.pallas_call(functools.partial(step_kernel, nlat), grid=(levels // per_...]
where the time goes in v4:
time: 41.4 us; the launch traced here: 41.3 us
  Pallas kernels  39.8 us (96%)
  other arithmetic  0.86 us (2%)
  between operations  0.64 us (2%)
    pallas_call x1, Pallas kernels, shards(): pl.pallas_call(functools.partial(exchange_kernel, axes, nlat, nlon), out_...  25.5 us
    pallas_call x1, Pallas kernels, shards(): pl.pallas_call(functools.partial(step_kernel, nlat), grid=(levels // per_...  14.3 us
    mul x1, other arithmetic, shards(): 0.5 * jnp.sin(math.pi * (global_rows + 0.5) / total_rows - 0.5 * math.pi)  0.86 us

profile of v4, /device:TPU:32, one launch (start us, length us, event | category | flops | bytes accessed | tf_op | source)
XLA Modules:
  0.0 41.3 jit_solution(2368158780949260691)
XLA Ops:
  0.6 0.9 %sine_multiply_fusion.f_ref = f32[128,1]{1,0:T(8,128)} fusion(s32[]{:T(128)S(6)} %mul.16), kind=kLoop, calls=%fused_computation | loop fusion | flops 768 | bytes 516 | tf_op jit(solution)/shard_map/mul | solution.py:285
  1.5 25.5 %shard_map.84 = (f32[4,16,2,128]{3,2,1,0:T(2,128)}, f32[4,16,2,128]{3,2,1,0:T(2,128)}, f32[4,16,2,128]{3,2,1,0:T(2,128)}, f32[4,16,2,128]{3,2,1,0:T(2,128)}, f32[4,2,8,128]{3,2,1,0:T(8,128)}) custom-call(f32[16,128,128]{2,1,0:T(8,128)} %t_ref.1, f32[16,128,128]{2,1,0:T(8,128)} %s_ref.1, f32[16,128,128]{2,1,0:T(8,128)} %u_ref.1, f32[16,128,128]{2,1,0:T(8,128)} %v_ref.1, ...), custom_call_target="tpu_custom_call" | custom-call | tf_op jit(solution)/shard_map/pallas_call | solution.py:269
  27.0 14.3 %shard_map.85 = (f32[16,128,128]{2,1,0:T(8,128)}, f32[16,128,128]{2,1,0:T(8,128)}, f32[16,128,128]{2,1,0:T(8,128)}, f32[16,128,128]{2,1,0:T(8,128)}) custom-call(f32[16,128,128]{2,1,0:T(8,128)} %t_ref.1, f32[16,128,128]{2,1,0:T(8,128)} %s_ref.1, f32[16,128,128]{2,1,0:T(8,128)} %u_ref.1, f32[16,128,128]{2,1,0:T(8,128)} %v_ref.1, s32[128,128]{1,0:T(8,128)} %d_ref.1, ...), custom_call_target="tpu_custom_call" | custom-call | tf_op jit(solution)/shard_map/pallas_call | solution.py:292

commit v5 on v4

--- a/solution.py
+++ b/solution.py
@@ -166,6 +166,9 @@
                 base, vp1, vm1, vp2, vm2, accx, accy, mt, tf):
     step = pl.program_id(0)
     per_step = t_ref.shape[0]
+    phases = (t_ref.shape[2] // 16) // per_step
+    grp = step // phases
+    phase = step % phases
     frame, width = base.shape[1], base.shape[2]
     rows = t_ref.shape[1]
     at_lat = lax.axis_index("lat")
@@ -193,17 +196,21 @@
             mt[0:2] = he_ref[n, k]
             mt[width - 2:width] = hw_ref[n, k]
             tf[top:top + rows] = jnp.transpose(mt[...])
-            slot = 16 * sub + 4 * n
-
-            def to_lane(line, src, dst):
-                return pltpu.roll(line, (dst - src) % width, 1)
-
-            sw_line = to_lane(cor_ref[0, step, 1:2], slot + 1, width - 1)
-            se_line = to_lane(cor_ref[1, step, 1:2], slot + 2, 0)
-            nw_line = to_lane(cor_ref[2, step, 0:1], slot + 1, width - 1)
-            ne_line = to_lane(cor_ref[3, step, 0:1], slot + 2, 0)
-            nw_raw = to_lane(cor_ref[2, step, 1:2], slot + 2, width - 1)
-            ne_raw = to_lane(cor_ref[3, step, 1:2], slot + 1, 0)
+            def to_lane(kind, row, off, dst):
+                line = cor_ref[kind, grp, row:row + 1]
+                picked = None
+                for ph in range(phases):
+                    slot = 16 * (ph * per_step + sub) + 4 * n
+                    moved = pltpu.roll(line, (dst - slot - off) % width, 1)
+                    picked = moved if picked is None else jnp.where(phase == ph, moved, picked)
+                return picked
+
+            sw_line = to_lane(0, 1, 1, width - 1)
+            se_line = to_lane(1, 1, 2, 0)
+            nw_line = to_lane(2, 0, 1, width - 1)
+            ne_line = to_lane(3, 0, 2, 0)
+            nw_raw = to_lane(2, 1, 2, width - 1)
+            ne_raw = to_lane(3, 1, 1, 0)
             low = jnp.where(line_lane == width - 1, sw_line, jnp.where(line_lane == 0, se_line, 0.0))
             high = jnp.where(line_lane == width - 1, nw_line, jnp.where(line_lane == 0, ne_line, 0.0))
             tf[top - 1:top] = jnp.where(south, low, 0.0)
@@ -285,7 +292,7 @@
     coriolis = (0.5 * jnp.sin(math.pi * (global_rows + 0.5) / total_rows - 0.5 * math.pi))[:, None]
 
     frame = rows_dev + 2 * top
-    per_step = cols_dev // 16
+    per_step = 4
     level_block = pl.BlockSpec((per_step, rows_dev, cols_dev), lambda k: (k, 0, 0))
     plane = pl.BlockSpec((rows_dev, cols_dev), lambda k: (0, 0))
     column = pl.BlockSpec((rows_dev, 1), lambda k: (0, 0))

time: 41.4 us -> 41.2 us (level)
  no operation moved by 1% of the time
where the time goes in v5:
time: 41.2 us; the launch traced here: 41.1 us
  Pallas kernels  39.6 us (96%)
  other arithmetic  0.86 us (2%)
  between operations  0.64 us (2%)
    pallas_call x1, Pallas kernels, shards(): pl.pallas_call(functools.partial(exchange_kernel, axes, nlat, nlon), out_...  25.5 us
    pallas_call x1, Pallas kernels, shards(): pl.pallas_call(functools.partial(step_kernel, nlat), grid=(levels // per_...  14.1 us
    mul x1, other arithmetic, shards(): 0.5 * jnp.sin(math.pi * (global_rows + 0.5) / total_rows - 0.5 * math.pi)  0.86 us

profile of v5, /device:TPU:32, one launch (start us, length us, event | category | flops | bytes accessed | tf_op | source)
XLA Modules:
  0.0 41.1 jit_solution(1179075038106213402)
XLA Ops:
  0.6 0.9 %sine_multiply_fusion.f_ref = f32[128,1]{1,0:T(8,128)} fusion(s32[]{:T(128)S(6)} %mul.16), kind=kLoop, calls=%fused_computation | loop fusion | flops 768 | bytes 516 | tf_op jit(solution)/shard_map/mul | solution.py:292
  1.5 25.5 %shard_map.84 = (f32[4,16,2,128]{3,2,1,0:T(2,128)}, f32[4,16,2,128]{3,2,1,0:T(2,128)}, f32[4,16,2,128]{3,2,1,0:T(2,128)}, f32[4,16,2,128]{3,2,1,0:T(2,128)}, f32[4,2,8,128]{3,2,1,0:T(8,128)}) custom-call(f32[16,128,128]{2,1,0:T(8,128)} %t_ref.1, f32[16,128,128]{2,1,0:T(8,128)} %s_ref.1, f32[16,128,128]{2,1,0:T(8,128)} %u_ref.1, f32[16,128,128]{2,1,0:T(8,128)} %v_ref.1, ...), custom_call_target="tpu_custom_call" | custom-call | tf_op jit(solution)/shard_map/pallas_call | solution.py:276
  27.0 14.1 %shard_map.85 = (f32[16,128,128]{2,1,0:T(8,128)}, f32[16,128,128]{2,1,0:T(8,128)}, f32[16,128,128]{2,1,0:T(8,128)}, f32[16,128,128]{2,1,0:T(8,128)}) custom-call(f32[16,128,128]{2,1,0:T(8,128)} %t_ref.1, f32[16,128,128]{2,1,0:T(8,128)} %s_ref.1, f32[16,128,128]{2,1,0:T(8,128)} %u_ref.1, f32[16,128,128]{2,1,0:T(8,128)} %v_ref.1, s32[128,128]{1,0:T(8,128)} %d_ref.1, ...), custom_call_target="tpu_custom_call" | custom-call | tf_op jit(solution)/shard_map/pallas_call | solution.py:299

commit v6 on v4

--- a/solution.py
+++ b/solution.py
@@ -45,10 +45,14 @@
     ne = (2 * nlon - 2 - b) % nlon
     nw = (nlon - b) % nlon
     fold = a == last
-    loads = [pltpu.make_async_copy(src, xin.at[n], in_sem.at[n])
-             for n, src in enumerate((t_hbm, s_hbm, u_hbm, v_hbm))]
-    loads.append(pltpu.make_async_copy(d_hbm, d_ref, in_sem.at[4]))
-    for copy in loads:
+    srcs = (t_hbm, s_hbm, u_hbm, v_hbm)
+    edges = [pltpu.make_async_copy(src.at[:, lo:lo + 8], xin.at[n, :, lo:lo + 8],
+                                   in_sem.at[2 * n + i])
+             for n, src in enumerate(srcs) for i, lo in enumerate((0, rows - 8))]
+    edges.append(pltpu.make_async_copy(d_hbm, d_ref, in_sem.at[8]))
+    middles = [pltpu.make_async_copy(src.at[:, 8:rows - 8], xin.at[n, :, 8:rows - 8],
+                                     in_sem.at[9 + n]) for n, src in enumerate(srcs)]
+    for copy in edges + middles:
         copy.start()
 
     def dev(la, lo):
@@ -73,16 +77,17 @@
         when(cond, lambda target=target: pl.semaphore_signal(
             barrier, 1, device_id=dev(*target), device_id_type=pl.DeviceIdType.MESH))
 
-    for copy in loads:
+    for copy in edges:
         copy.wait()
 
     def rows_body(k, carry):
         wet = jnp.where(d_ref[...] > k, 1.0, 0.0).astype(jnp.float32)
         for n in range(4):
-            x = xin[n, k] * wet
-            top_b[n, k] = x[0:2]
-            bot_b[n, k] = x[rows - 2:rows]
-            flipped = reverse_lanes(x[rows - 8:rows])
+            x_top = xin[n, k, 0:8] * wet[0:8]
+            x_bot = xin[n, k, rows - 8:rows] * wet[rows - 8:rows]
+            top_b[n, k] = x_top[0:2]
+            bot_b[n, k] = x_bot[6:8]
+            flipped = reverse_lanes(x_bot)
             fold_b[n, k, 0:1] = signs[n] * flipped[7:8]
             fold_b[n, k, 1:2] = signs[n] * flipped[6:7]
         return carry
@@ -137,6 +142,8 @@
     copies = []
     for idx, (send, recv, src, dst, target) in enumerate(relations):
         if idx == 3:
+            for copy in middles:
+                copy.wait()
             lax.fori_loop(0, levels // group, cols_body, 0)
         copy = pltpu.make_async_remote_copy(
             src_ref=src, dst_ref=dst, send_sem=send_sem.at[idx], recv_sem=recv_sem.at[idx],
@@ -276,7 +283,7 @@
         + [pltpu.VMEM(strip.shape, f32)] * 9
         + [pltpu.VMEM(corners.shape[1:], f32), pltpu.VMEM(corners.shape, f32)]
         + [pltpu.SemaphoreType.DMA((11,)), pltpu.SemaphoreType.DMA((11,)),
-           pltpu.SemaphoreType.DMA((5,)), pltpu.SemaphoreType.DMA((2,))],
+           pltpu.SemaphoreType.DMA((13,)), pltpu.SemaphoreType.DMA((2,))],
         compiler_params=pltpu.CompilerParams(collective_id=0, has_side_effects=True),
     )(temp, salt, uvel, vvel, depth_levels)
 

time: 41.4 us -> 40.4 us (0.976)
  Pallas kernels: 39.8 us -> 38.8 us
    pallas_call x1, Pallas kernels: 25.5 us -> 24.5 us  [shards(): pl.pallas_call(functools.partial(exchange_kernel, axes, nlat, nlon), out_...]
where the time goes in v6:
time: 40.4 us; the launch traced here: 40.3 us
  Pallas kernels  38.8 us (96%)
  other arithmetic  0.86 us (2%)
  between operations  0.64 us (2%)
    pallas_call x1, Pallas kernels, shards(): pl.pallas_call(functools.partial(exchange_kernel, axes, nlat, nlon), out_...  24.5 us
    pallas_call x1, Pallas kernels, shards(): pl.pallas_call(functools.partial(step_kernel, nlat), grid=(levels // per_...  14.3 us
    mul x1, other arithmetic, shards(): 0.5 * jnp.sin(math.pi * (global_rows + 0.5) / total_rows - 0.5 * math.pi)  0.86 us

profile of v6, /device:TPU:32, one launch (start us, length us, event | category | flops | bytes accessed | tf_op | source)
XLA Modules:
  0.0 40.3 jit_solution(7293497620099133904)
XLA Ops:
  0.6 0.9 %sine_multiply_fusion.f_ref = f32[128,1]{1,0:T(8,128)} fusion(s32[]{:T(128)S(6)} %mul.16), kind=kLoop, calls=%fused_computation | loop fusion | flops 768 | bytes 516 | tf_op jit(solution)/shard_map/mul | solution.py:292
  1.5 24.5 %shard_map.84 = (f32[4,16,2,128]{3,2,1,0:T(2,128)}, f32[4,16,2,128]{3,2,1,0:T(2,128)}, f32[4,16,2,128]{3,2,1,0:T(2,128)}, f32[4,16,2,128]{3,2,1,0:T(2,128)}, f32[4,2,8,128]{3,2,1,0:T(8,128)}) custom-call(f32[16,128,128]{2,1,0:T(8,128)} %t_ref.1, f32[16,128,128]{2,1,0:T(8,128)} %s_ref.1, f32[16,128,128]{2,1,0:T(8,128)} %u_ref.1, f32[16,128,128]{2,1,0:T(8,128)} %v_ref.1, ...), custom_call_target="tpu_custom_call" | custom-call | tf_op jit(solution)/shard_map/pallas_call | solution.py:276
  26.0 14.3 %shard_map.85 = (f32[16,128,128]{2,1,0:T(8,128)}, f32[16,128,128]{2,1,0:T(8,128)}, f32[16,128,128]{2,1,0:T(8,128)}, f32[16,128,128]{2,1,0:T(8,128)}) custom-call(f32[16,128,128]{2,1,0:T(8,128)} %t_ref.1, f32[16,128,128]{2,1,0:T(8,128)} %s_ref.1, f32[16,128,128]{2,1,0:T(8,128)} %u_ref.1, f32[16,128,128]{2,1,0:T(8,128)} %v_ref.1, s32[128,128]{1,0:T(8,128)} %d_ref.1, ...), custom_call_target="tpu_custom_call" | custom-call | tf_op jit(solution)/shard_map/pallas_call | solution.py:299

commit v7 on v6

--- a/solution.py
+++ b/solution.py
@@ -126,12 +126,13 @@
     peers = 2 + 3 * below + 3 * above + at_fold * (1 + ne_apart + nw_apart)
     pl.semaphore_wait(barrier, peers)
 
-    relations = [
+    ngroups = levels // group
+    rows_rel = [
         (a < last, a > 0, bot_b, hs, (a + 1, b)),
         (a > 0, a < last, top_b, hn, (a - 1, b)),
         (fold, fold, fold_b, hn, (last, mirror)),
-        (True, True, lft_b, he, (a, left)),
-        (True, True, rgt_b, hw, (a, right)),
+    ]
+    corner_rel = [
         (a < last, a > 0, csrc, cor.at[0], (a + 1, right)),
         (a < last, a > 0, csrc, cor.at[1], (a + 1, left)),
         (a > 0, a < last, csrc, cor.at[2], (a - 1, right)),
@@ -140,16 +141,27 @@
         (fold & (nw != b), fold & (nw != b), csrc, cor.at[2], (last, nw)),
     ]
     copies = []
-    for idx, (send, recv, src, dst, target) in enumerate(relations):
-        if idx == 3:
-            for copy in middles:
-                copy.wait()
-            lax.fori_loop(0, levels // group, cols_body, 0)
-        copy = pltpu.make_async_remote_copy(
-            src_ref=src, dst_ref=dst, send_sem=send_sem.at[idx], recv_sem=recv_sem.at[idx],
-            device_id=dev(*target), device_id_type=pl.DeviceIdType.MESH)
-        copies.append((send, recv, copy))
-        when(send, copy.start)
+
+    def send_all(relations):
+        for send, recv, src, dst, target in relations:
+            idx = len(copies)
+            copy = pltpu.make_async_remote_copy(
+                src_ref=src, dst_ref=dst, send_sem=send_sem.at[idx], recv_sem=recv_sem.at[idx],
+                device_id=dev(*target), device_id_type=pl.DeviceIdType.MESH)
+            copies.append((send, recv, copy))
+            when(send, copy.start)
+
+    send_all(rows_rel)
+    for copy in middles:
+        copy.wait()
+    for g in range(ngroups):
+        cols_body(g, 0)
+        span = slice(g * group, (g + 1) * group)
+        send_all([
+            (True, True, lft_b.at[:, span], he.at[:, span], (a, left)),
+            (True, True, rgt_b.at[:, span], hw.at[:, span], (a, right)),
+        ])
+    send_all(corner_rel)
     own = [
         (fold & (ne == b), pltpu.make_async_copy(csrc, cor.at[3], local_sem.at[0])),
         (fold & (nw == b), pltpu.make_async_copy(csrc, cor.at[2], local_sem.at[1])),
@@ -282,7 +294,8 @@
                         pltpu.VMEM(depth_levels.shape, jnp.int32)]
         + [pltpu.VMEM(strip.shape, f32)] * 9
         + [pltpu.VMEM(corners.shape[1:], f32), pltpu.VMEM(corners.shape, f32)]
-        + [pltpu.SemaphoreType.DMA((11,)), pltpu.SemaphoreType.DMA((11,)),
+        + [pltpu.SemaphoreType.DMA((9 + levels * 32 // cols_dev,)),
+           pltpu.SemaphoreType.DMA((9 + levels * 32 // cols_dev,)),
            pltpu.SemaphoreType.DMA((13,)), pltpu.SemaphoreType.DMA((2,))],
         compiler_params=pltpu.CompilerParams(collective_id=0, has_side_effects=True),
     )(temp, salt, uvel, vvel, depth_levels)

time: 40.4 us -> 40.4 us (level)
  no operation moved by 1% of the time
where the time goes in v7:
time: 40.4 us; the launch traced here: 40.3 us
  Pallas kernels  38.8 us (96%)
  other arithmetic  0.86 us (2%)
  between operations  0.64 us (2%)
    pallas_call x1, Pallas kernels, shards(): pl.pallas_call(functools.partial(exchange_kernel, axes, nlat, nlon), out_...  24.5 us
    pallas_call x1, Pallas kernels, shards(): pl.pallas_call(functools.partial(step_kernel, nlat), grid=(levels // per_...  14.3 us
    mul x1, other arithmetic, shards(): 0.5 * jnp.sin(math.pi * (global_rows + 0.5) / total_rows - 0.5 * math.pi)  0.86 us

profile of v7, /device:TPU:32, one launch (start us, length us, event | category | flops | bytes accessed | tf_op | source)
XLA Modules:
  0.0 40.3 jit_solution(6509738658197264529)
XLA Ops:
  0.6 0.9 %sine_multiply_fusion.f_ref = f32[128,1]{1,0:T(8,128)} fusion(s32[]{:T(128)S(6)} %mul.16), kind=kLoop, calls=%fused_computation | loop fusion | flops 768 | bytes 516 | tf_op jit(solution)/shard_map/mul | solution.py:305
  1.5 24.5 %shard_map.84 = (f32[4,16,2,128]{3,2,1,0:T(2,128)}, f32[4,16,2,128]{3,2,1,0:T(2,128)}, f32[4,16,2,128]{3,2,1,0:T(2,128)}, f32[4,16,2,128]{3,2,1,0:T(2,128)}, f32[4,2,8,128]{3,2,1,0:T(8,128)}) custom-call(f32[16,128,128]{2,1,0:T(8,128)} %t_ref.1, f32[16,128,128]{2,1,0:T(8,128)} %s_ref.1, f32[16,128,128]{2,1,0:T(8,128)} %u_ref.1, f32[16,128,128]{2,1,0:T(8,128)} %v_ref.1, ...), custom_call_target="tpu_custom_call" | custom-call | tf_op jit(solution)/shard_map/pallas_call | solution.py:288
  26.0 14.3 %shard_map.85 = (f32[16,128,128]{2,1,0:T(8,128)}, f32[16,128,128]{2,1,0:T(8,128)}, f32[16,128,128]{2,1,0:T(8,128)}, f32[16,128,128]{2,1,0:T(8,128)}) custom-call(f32[16,128,128]{2,1,0:T(8,128)} %t_ref.1, f32[16,128,128]{2,1,0:T(8,128)} %s_ref.1, f32[16,128,128]{2,1,0:T(8,128)} %u_ref.1, f32[16,128,128]{2,1,0:T(8,128)} %v_ref.1, s32[128,128]{1,0:T(8,128)} %d_ref.1, ...), custom_call_target="tpu_custom_call" | custom-call | tf_op jit(solution)/shard_map/pallas_call | solution.py:312

commit v8 on v5

--- a/solution.py
+++ b/solution.py
@@ -45,10 +45,14 @@
     ne = (2 * nlon - 2 - b) % nlon
     nw = (nlon - b) % nlon
     fold = a == last
-    loads = [pltpu.make_async_copy(src, xin.at[n], in_sem.at[n])
-             for n, src in enumerate((t_hbm, s_hbm, u_hbm, v_hbm))]
-    loads.append(pltpu.make_async_copy(d_hbm, d_ref, in_sem.at[4]))
-    for copy in loads:
+    srcs = (t_hbm, s_hbm, u_hbm, v_hbm)
+    edges = [pltpu.make_async_copy(src.at[:, lo:lo + 8], xin.at[n, :, lo:lo + 8],
+                                   in_sem.at[2 * n + i])
+             for n, src in enumerate(srcs) for i, lo in enumerate((0, rows - 8))]
+    edges.append(pltpu.make_async_copy(d_hbm, d_ref, in_sem.at[8]))
+    middles = [pltpu.make_async_copy(src.at[:, 8:rows - 8], xin.at[n, :, 8:rows - 8],
+                                     in_sem.at[9 + n]) for n, src in enumerate(srcs)]
+    for copy in edges + middles:
         copy.start()
 
     def dev(la, lo):
@@ -73,16 +77,17 @@
         when(cond, lambda target=target: pl.semaphore_signal(
             barrier, 1, device_id=dev(*target), device_id_type=pl.DeviceIdType.MESH))
 
-    for copy in loads:
+    for copy in edges:
         copy.wait()
 
     def rows_body(k, carry):
         wet = jnp.where(d_ref[...] > k, 1.0, 0.0).astype(jnp.float32)
         for n in range(4):
-            x = xin[n, k] * wet
-            top_b[n, k] = x[0:2]
-            bot_b[n, k] = x[rows - 2:rows]
-            flipped = reverse_lanes(x[rows - 8:rows])
+            x_top = xin[n, k, 0:8] * wet[0:8]
+            x_bot = xin[n, k, rows - 8:rows] * wet[rows - 8:rows]
+            top_b[n, k] = x_top[0:2]
+            bot_b[n, k] = x_bot[6:8]
+            flipped = reverse_lanes(x_bot)
             fold_b[n, k, 0:1] = signs[n] * flipped[7:8]
             fold_b[n, k, 1:2] = signs[n] * flipped[6:7]
         return carry
@@ -137,6 +142,8 @@
     copies = []
     for idx, (send, recv, src, dst, target) in enumerate(relations):
         if idx == 3:
+            for copy in middles:
+                copy.wait()
             lax.fori_loop(0, levels // group, cols_body, 0)
         copy = pltpu.make_async_remote_copy(
             src_ref=src, dst_ref=dst, send_sem=send_sem.at[idx], recv_sem=recv_sem.at[idx],
@@ -283,7 +290,7 @@
         + [pltpu.VMEM(strip.shape, f32)] * 9
         + [pltpu.VMEM(corners.shape[1:], f32), pltpu.VMEM(corners.shape, f32)]
         + [pltpu.SemaphoreType.DMA((11,)), pltpu.SemaphoreType.DMA((11,)),
-           pltpu.SemaphoreType.DMA((5,)), pltpu.SemaphoreType.DMA((2,))],
+           pltpu.SemaphoreType.DMA((13,)), pltpu.SemaphoreType.DMA((2,))],
         compiler_params=pltpu.CompilerParams(collective_id=0, has_side_effects=True),
     )(temp, salt, uvel, vvel, depth_levels)
 

time: 41.2 us -> 40.2 us (0.976)
  Pallas kernels: 39.6 us -> 38.6 us
    pallas_call x1, Pallas kernels: 25.5 us -> 24.5 us  [shards(): pl.pallas_call(functools.partial(exchange_kernel, axes, nlat, nlon), out_...]
where the time goes in v8:
time: 40.2 us; the launch traced here: 40.1 us
  Pallas kernels  38.6 us (96%)
  other arithmetic  0.86 us (2%)
  between operations  0.64 us (2%)
    pallas_call x1, Pallas kernels, shards(): pl.pallas_call(functools.partial(exchange_kernel, axes, nlat, nlon), out_...  24.5 us
    pallas_call x1, Pallas kernels, shards(): pl.pallas_call(functools.partial(step_kernel, nlat), grid=(levels // per_...  14.1 us
    mul x1, other arithmetic, shards(): 0.5 * jnp.sin(math.pi * (global_rows + 0.5) / total_rows - 0.5 * math.pi)  0.86 us

profile of v8, /device:TPU:32, one launch (start us, length us, event | category | flops | bytes accessed | tf_op | source)
XLA Modules:
  0.0 40.1 jit_solution(15536287125884218870)
XLA Ops:
  0.6 0.9 %sine_multiply_fusion.f_ref = f32[128,1]{1,0:T(8,128)} fusion(s32[]{:T(128)S(6)} %mul.16), kind=kLoop, calls=%fused_computation | loop fusion | flops 768 | bytes 516 | tf_op jit(solution)/shard_map/mul | solution.py:299
  1.5 24.5 %shard_map.84 = (f32[4,16,2,128]{3,2,1,0:T(2,128)}, f32[4,16,2,128]{3,2,1,0:T(2,128)}, f32[4,16,2,128]{3,2,1,0:T(2,128)}, f32[4,16,2,128]{3,2,1,0:T(2,128)}, f32[4,2,8,128]{3,2,1,0:T(8,128)}) custom-call(f32[16,128,128]{2,1,0:T(8,128)} %t_ref.1, f32[16,128,128]{2,1,0:T(8,128)} %s_ref.1, f32[16,128,128]{2,1,0:T(8,128)} %u_ref.1, f32[16,128,128]{2,1,0:T(8,128)} %v_ref.1, ...), custom_call_target="tpu_custom_call" | custom-call | tf_op jit(solution)/shard_map/pallas_call | solution.py:283
  26.0 14.1 %shard_map.85 = (f32[16,128,128]{2,1,0:T(8,128)}, f32[16,128,128]{2,1,0:T(8,128)}, f32[16,128,128]{2,1,0:T(8,128)}, f32[16,128,128]{2,1,0:T(8,128)}) custom-call(f32[16,128,128]{2,1,0:T(8,128)} %t_ref.1, f32[16,128,128]{2,1,0:T(8,128)} %s_ref.1, f32[16,128,128]{2,1,0:T(8,128)} %u_ref.1, f32[16,128,128]{2,1,0:T(8,128)} %v_ref.1, s32[128,128]{1,0:T(8,128)} %d_ref.1, ...), custom_call_target="tpu_custom_call" | custom-call | tf_op jit(solution)/shard_map/pallas_call | solution.py:306
